TPU v7x, 32 devices: a whole 2x2x4 slice. The times are simulated.
32 devices in a mesh: dp: 8 (over z, core), fsdp: 4 (over y, x).
Axes of the slice: x: 2, y: 2, z: 4, core: 2. Of those that a mesh axis runs over, the one named last changes fastest.
Arguments:
- pixels: bfloat16 [32768, 768], P(('dp', 'fsdp')), may hold values from -6 to 6
- valid_mask: int32 [32768, 768], P(('dp', 'fsdp')), may hold values from 0 to 1
- size_groups: int32 [32], P(('dp', 'fsdp')), may hold values from 0 to 2
- code_index: int32 [4, 8192], P(None, ('dp', 'fsdp')), may hold values from 0 to 16383, as said below
- w_pixel: float32 [2, 768, 512], P(None, 'fsdp', 'dp'), may hold values from -0.625 to 0.625
- w_res: float32 [4, 4608, 512], P(None, 'fsdp', 'dp'), may hold values from -0.1875 to 0.1875
- w_scale: float32 [2, 2048, 512], P(None, 'fsdp', 'dp'), may hold values from -0.5 to 0.5
- w_latent: float32 [2, 512, 256], P(None, 'fsdp', 'dp'), may hold values from -0.75 to 0.75
- norm_gains: float32 [8, 512], replicated, may hold values from -0.9 to 1.5
- moment_pixel: float32 [2, 768, 512], P(None, 'fsdp', 'dp'), may hold values from -4.4703484e-08 to 4.4703484e-08
- moment_res: float32 [4, 4608, 512], P(None, 'fsdp', 'dp'), may hold values from -4.4703484e-08 to 4.4703484e-08
- moment_scale: float32 [2, 2048, 512], P(None, 'fsdp', 'dp'), may hold values from -4.4703484e-08 to 4.4703484e-08
- moment_latent: float32 [2, 512, 256], P(None, 'fsdp', 'dp'), may hold values from -4.4703484e-08 to 4.4703484e-08
- moment_gains: float32 [8, 512], replicated, may hold values from -1.4901161e-07 to 1.4901161e-07
- second_pixel: float32 [2, 768, 512], P(None, 'fsdp', 'dp'), may hold values from 7.84e-18 to 3.136e-17
- second_res: float32 [4, 4608, 512], P(None, 'fsdp', 'dp'), may hold values from 7.84e-18 to 3.136e-17
- second_scale: float32 [2, 2048, 512], P(None, 'fsdp', 'dp'), may hold values from 7.84e-18 to 3.136e-17
- second_latent: float32 [2, 512, 256], P(None, 'fsdp', 'dp'), may hold values from 7.84e-18 to 3.136e-17
- second_gains: float32 [8, 512], replicated, may hold values from 1e-16 to 4e-16
- ema_counts: float32 [16384], P(('dp', 'fsdp')), may hold values from 0.5 to 4
- ema_sums: float32 [16384, 256], P(('dp', 'fsdp')), may hold values from -6 to 6
Outputs:
- loss_parts: float32 [3], replicated
- grad_norm: float32 [1], replicated
- next_pixel: float32 [2, 768, 512], P(None, 'fsdp', 'dp')
- next_moment_pixel: float32 [2, 768, 512], P(None, 'fsdp', 'dp')
- next_second_pixel: float32 [2, 768, 512], P(None, 'fsdp', 'dp')
- copy_pixel: bfloat16 [2, 768, 512], P(None, 'fsdp', 'dp')
- next_res: float32 [4, 4608, 512], P(None, 'fsdp', 'dp')
- next_moment_res: float32 [4, 4608, 512], P(None, 'fsdp', 'dp')
- next_second_res: float32 [4, 4608, 512], P(None, 'fsdp', 'dp')
- copy_res: bfloat16 [4, 4608, 512], P(None, 'fsdp', 'dp')
- next_scale: float32 [2, 2048, 512], P(None, 'fsdp', 'dp')
- next_moment_scale: float32 [2, 2048, 512], P(None, 'fsdp', 'dp')
- next_second_scale: float32 [2, 2048, 512], P(None, 'fsdp', 'dp')
- copy_scale: bfloat16 [2, 2048, 512], P(None, 'fsdp', 'dp')
- next_latent: float32 [2, 512, 256], P(None, 'fsdp', 'dp')
- next_moment_latent: float32 [2, 512, 256], P(None, 'fsdp', 'dp')
- next_second_latent: float32 [2, 512, 256], P(None, 'fsdp', 'dp')
- copy_latent: bfloat16 [2, 512, 256], P(None, 'fsdp', 'dp')
- next_gains: float32 [8, 512], replicated
- next_moment_gains: float32 [8, 512], replicated
- next_second_gains: float32 [8, 512], replicated
- next_counts: float32 [16384], P(('dp', 'fsdp'))
- next_sums: float32 [16384, 256], P(('dp', 'fsdp'))
- codebook: float32 [16384, 256], P(('dp', 'fsdp'))
- codebook_copy: bfloat16 [16384, 256], P(('dp', 'fsdp'))
Inputs may be any that keep to these rules, and one draw needn't show every extreme that they name: `code_index`: among the 4 x 256 codes of one device's positions, at most 64 lie in any one device's block of 16384 / 32 consecutive codes, and on every device some block holds exactly 64 of them.
All inputs are finite; a program needn't handle non-finite values.
Results may differ from a plain program's by a relative error of at most 0.0061.
Values may be sent and summed in bfloat16 or wider, within the bound.
No kernel may reach another device: no remote copies, remote signals or barrier semaphores. Data moves between devices by JAX's collectives and lax.ppermute only.
A program may use at most 256 MiB of HBM per device.

v0:
```python
import jax
import jax.numpy as jnp
from jax import lax
from jax.sharding import PartitionSpec as P

C = 512
ZD = 256
K = 16384
GROUPS = 32
SIDE = 32
DEPTH = 4
STEP = 5
HIGH = lax.Precision.HIGHEST
TAPS = [(dy, dx) for dy in (-1, 0, 1) for dx in (-1, 0, 1)]
COMMIT_WEIGHT = 0.25
CLIP_AT = 1e-05
EMA_DECAY = 0.8
WEIGHT_RATE = 0.03
GAIN_RATE = 0.4


def geometry(groups, size, width):
    span = jnp.left_shift(jnp.ones_like(groups), groups)
    sides = size // 4 * span
    tile = jnp.arange(16, dtype=jnp.int32)[None, :]
    image = tile // 4 // span[:, None] * (4 // span[:, None]) + tile % 4 // span[:, None]
    member = (image[:, :, None] == jnp.arange(16, dtype=jnp.int32)[None, None, :]).astype(
        jnp.float32
    )
    count = (sides * sides).astype(jnp.float32) * (width // GROUPS)
    return (sides, member, count)


def image_means(field, member, count):
    batch, size, _, width = field.shape
    tile = size // 4
    sums = jnp.sum(field.reshape(batch, 4, tile, 4, tile, width), axis=(2, 4)).reshape(
        batch, 16, width
    )
    per_image = jnp.einsum("btm,btc->bmc", member, sums, precision=HIGH)
    grouped = (
        jnp.sum(per_image.reshape(batch, 16, GROUPS, width // GROUPS), axis=3)
        / count[:, None, None]
    )
    spread = jnp.einsum("btm,bmg->btg", member, grouped, precision=HIGH)
    full = jnp.repeat(spread, width // GROUPS, axis=2).reshape(batch, 4, 1, 4, 1, width)
    return jnp.broadcast_to(full, (batch, 4, tile, 4, tile, width)).reshape(
        batch, size, size, width
    )


def gn_silu(field, gamma, beta, geom):
    mean = image_means(field, geom[1], geom[2])
    centered = field - mean
    var = image_means(centered * centered, geom[1], geom[2])
    return jax.nn.silu(centered * lax.rsqrt(var + 1e-05) * gamma + beta)


def silu_slope(value):
    gate = jax.nn.sigmoid(value)
    return gate * (1.0 + value * (1.0 - gate))


def side_masks(sides, size, delta):
    pos = jnp.arange(size, dtype=jnp.int32)
    near = pos + delta
    inside = (near >= 0) & (near < size)
    same = near[None, :] // sides[:, None] == pos[None, :] // sides[:, None]
    return (inside[None, :] & same).astype(jnp.float32)


def shifted(act, sides, dy, dx):
    size = act.shape[1]
    padded = jnp.pad(act, ((0, 0), (1, 1), (1, 1), (0, 0)))
    part = padded[:, 1 + dy : 1 + dy + size, 1 + dx : 1 + dx + size, :]
    keep = side_masks(sides, size, dy)[:, :, None] * side_masks(sides, size, dx)[:, None, :]
    return part * keep[..., None].astype(act.dtype)


def along_rows(left, right):
    return lax.dot_general(
        left, right, (((0,), (0,)), ((), ())), preferred_element_type=jnp.float32
    )


def along_cols(left, right):
    return lax.dot_general(
        left, right, (((1,), (1,)), ((), ())), preferred_element_type=jnp.float32
    )


def conv_forward(act, taps, geom):
    width = act.shape[3]
    total = jnp.zeros((act.shape[0] * act.shape[1] * act.shape[2], width), jnp.float32)
    for index, (dy, dx) in enumerate(TAPS):
        piece = shifted(act, geom[0], dy, dx).reshape(-1, width)
        total = total + jnp.dot(piece, taps[index], preferred_element_type=jnp.float32)
    return total.reshape(act.shape)


def conv_backward(act, taps, grad_out, geom):
    width = act.shape[3]
    grad_low = grad_out.reshape(-1, width).astype(jnp.bfloat16)
    weight_parts = []
    grad_act = jnp.zeros(act.shape, jnp.float32)
    for index, (dy, dx) in enumerate(TAPS):
        piece = shifted(act, geom[0], dy, dx).reshape(-1, width)
        weight_parts.append(along_rows(piece, grad_low))
        back = along_cols(grad_low, taps[index]).reshape(act.shape)
        grad_act = grad_act + shifted(back, geom[0], -dy, -dx)
    return (jnp.concatenate(weight_parts, axis=0), grad_act)


def block_forward(field, taps_pair, gains, first, geom):
    a_one = gn_silu(field, gains[first], gains[4 + first], geom).astype(jnp.bfloat16)
    t_one = conv_forward(a_one, taps_pair[0], geom)
    a_two = gn_silu(t_one, gains[first + 1], gains[5 + first], geom).astype(jnp.bfloat16)
    t_two = conv_forward(a_two, taps_pair[1], geom)
    return (field + t_two, (field, a_one, t_one, a_two))


def block_backward(grad, kept, taps_pair, gains, first, geom):
    field, a_one, t_one, a_two = kept
    grad_two, d_a_two = conv_backward(a_two, taps_pair[1], grad, geom)
    _, pull = jax.vjp(
        lambda x, g, b: gn_silu(x, g, b, geom), t_one, gains[first + 1], gains[5 + first]
    )
    d_t_one, scale_two, shift_two = pull(d_a_two)
    grad_one, d_a_one = conv_backward(a_one, taps_pair[0], d_t_one, geom)
    _, pull = jax.vjp(lambda x, g, b: gn_silu(x, g, b, geom), field, gains[first], gains[4 + first])
    d_field, scale_one, shift_one = pull(d_a_one)
    return (grad + d_field, (grad_one, grad_two), (scale_one, scale_two, shift_one, shift_two))


def to_depth(field):
    batch, size, _, width = field.shape
    half = size // 2
    parts = field.reshape(batch, half, 2, half, 2, width).transpose(0, 1, 3, 2, 4, 5)
    return parts.reshape(batch * half * half, 4 * width)


def from_depth(rows, batch, size):
    half = size // 2
    width = rows.shape[1] // 4
    parts = rows.reshape(batch, half, half, 2, 2, width).transpose(0, 1, 3, 2, 4, 5)
    return parts.reshape(batch, size, size, width)


def fetch(shard):
    cols = lax.all_gather(shard.astype(jnp.bfloat16), "dp", axis=1, tiled=True)
    return lax.all_gather(cols, "fsdp", axis=0, tiled=True)


def backward_copy(shard, ready):
    return fetch(shard).reshape(ready.shape)


def reduce_grad(full):
    rows = lax.psum_scatter(full, "fsdp", scatter_dimension=0, tiled=True)
    return lax.psum_scatter(rows, "dp", scatter_dimension=1, tiled=True)


def adam_step(weight, moment, second, grad, rate):
    moment_new = 0.5 * moment + 0.5 * grad
    second_new = 0.5 * second + 0.5 * grad * grad
    fix = 1.0 - 0.5**STEP
    weight_new = weight - rate * (
        moment_new / fix / (jnp.sqrt(second_new / fix) + 1e-12) + 0.01 * weight
    )
    return (weight_new, moment_new, second_new)


def owner_slots(flat_codes, devices, capacity, rows_own):
    owner = flat_codes // rows_own
    order = jnp.argsort(owner, stable=True)
    ranked = owner[order]
    first = jnp.searchsorted(ranked, jnp.arange(devices, dtype=jnp.int32))
    place = jnp.arange(flat_codes.shape[0], dtype=jnp.int32) - first[ranked]
    return jnp.zeros_like(flat_codes).at[order].set(ranked * capacity + place)


def on_device(
    pixels,
    valid_mask,
    size_groups,
    code_index,
    w_pixel,
    w_res,
    w_scale,
    w_latent,
    norm_gains,
    moment_pixel,
    moment_res,
    moment_scale,
    moment_latent,
    moment_gains,
    second_pixel,
    second_res,
    second_scale,
    second_latent,
    second_gains,
    ema_counts,
    ema_sums,
):
    canv = size_groups.shape[0]
    n_outer = lax.axis_size("dp")
    n_inner = lax.axis_size("fsdp")
    devices = n_outer * n_inner
    latent_all = code_index.shape[1] * devices
    rows = ema_sums.shape[0]
    flat_codes = code_index.reshape(-1)
    capacity = max(2, 2 * flat_codes.shape[0] // devices)
    slot = owner_slots(flat_codes, devices, capacity, rows)
    local_row = flat_codes % rows
    geom = geometry(size_groups, SIDE, C)
    mask = valid_mask.astype(jnp.float32)
    total_valid = lax.psum(jnp.sum(mask), ("dp", "fsdp"))
    book = (ema_sums / ema_counts[:, None]).astype(jnp.bfloat16)
    wanted = jnp.full((devices * capacity,), -1, jnp.int32).at[slot].set(local_row)
    wanted = wanted.reshape(n_outer, n_inner, capacity)
    asked = lax.all_to_all(
        lax.all_to_all(wanted, "dp", split_axis=0, concat_axis=0, tiled=True),
        "fsdp",
        split_axis=1,
        concat_axis=1,
        tiled=True,
    )
    answer = jnp.take(book, jnp.maximum(asked, 0), axis=0)
    replies = lax.all_to_all(
        lax.all_to_all(answer, "dp", split_axis=0, concat_axis=0, tiled=True),
        "fsdp",
        split_axis=1,
        concat_axis=1,
        tiled=True,
    )
    picked_rows = replies.reshape(devices * capacity, -1)[slot].reshape(
        code_index.shape + (book.shape[1],)
    )
    q_cum = jnp.cumsum(picked_rows.astype(jnp.float32), axis=0)
    patch_in = fetch(w_pixel[0])
    field = jnp.dot(pixels, patch_in, preferred_element_type=jnp.float32).reshape(
        canv, SIDE, SIDE, C
    )
    enc_taps = (fetch(w_res[0]).reshape(9, C, C), fetch(w_res[1]).reshape(9, C, C))
    field, kept_enc = block_forward(field, enc_taps, norm_gains, 0, geom)
    e_four = to_depth(field.astype(jnp.bfloat16))
    w_down = fetch(w_scale[0])
    hidden = jnp.dot(e_four, w_down, preferred_element_type=jnp.float32)
    s_one = jax.nn.silu(hidden).astype(jnp.bfloat16)
    w_proj = fetch(w_latent[0])
    latent = jnp.dot(s_one, w_proj, preferred_element_type=jnp.float32)
    diff = latent[None] - q_cum
    commit = jnp.sum(diff * diff)
    shift = q_cum[DEPTH - 1] - latent
    quant = (latent + shift).astype(jnp.bfloat16)
    w_back = fetch(w_latent[1])
    inner = along_cols(quant, w_back)
    s_two = jax.nn.silu(inner).astype(jnp.bfloat16)
    w_up = fetch(w_scale[1])
    upper = along_cols(s_two, w_up)
    dec_field = from_depth(upper, canv, SIDE)
    dec_taps = (fetch(w_res[2]).reshape(9, C, C), fetch(w_res[3]).reshape(9, C, C))
    dec_field, kept_dec = block_forward(dec_field, dec_taps, norm_gains, 2, geom)
    outer = jax.nn.silu(dec_field).astype(jnp.bfloat16).reshape(-1, C)
    w_head = fetch(w_pixel[1])
    recon = along_cols(outer, w_head)
    err = recon - pixels.astype(jnp.float32)
    smooth = jnp.sqrt(err * err + 1.0)
    l1_local = jnp.sum(mask * (smooth - 1.0))
    grad_rec = (mask * err / smooth / total_valid).astype(jnp.bfloat16)
    d_head = along_rows(grad_rec, outer)
    head_b = backward_copy(w_pixel[1], w_head)
    d_outer = jnp.dot(grad_rec, head_b, preferred_element_type=jnp.float32)
    d_dec = (d_outer * silu_slope(dec_field.reshape(-1, C))).reshape(dec_field.shape)
    dec_b = (backward_copy(w_res[2], dec_taps[0]), backward_copy(w_res[3], dec_taps[1]))
    d_dec, dec_grads, dec_gain = block_backward(d_dec, kept_dec, dec_b, norm_gains, 2, geom)
    d_upper = to_depth(d_dec).astype(jnp.bfloat16)
    d_up = along_rows(d_upper, s_two)
    up_b = backward_copy(w_scale[1], w_up)
    d_s_two = jnp.dot(d_upper, up_b, preferred_element_type=jnp.float32)
    d_inner = (d_s_two * silu_slope(inner)).astype(jnp.bfloat16)
    d_back = along_rows(d_inner, quant)
    back_b = backward_copy(w_latent[1], w_back)
    d_quant = jnp.dot(d_inner, back_b, preferred_element_type=jnp.float32)
    d_latent = d_quant + 2.0 * COMMIT_WEIGHT / (latent_all * ZD) * jnp.sum(diff, axis=0)
    d_latent = d_latent.astype(jnp.bfloat16)
    d_proj = along_rows(s_one, d_latent)
    proj_b = backward_copy(w_latent[0], w_proj)
    d_s_one = along_cols(d_latent, proj_b)
    d_hidden = (d_s_one * silu_slope(hidden)).astype(jnp.bfloat16)
    d_down = along_rows(e_four, d_hidden)
    down_b = backward_copy(w_scale[0], w_down)
    d_e_four = along_cols(d_hidden, down_b)
    d_enc = from_depth(d_e_four, canv, SIDE)
    enc_b = (backward_copy(w_res[0], enc_taps[0]), backward_copy(w_res[1], enc_taps[1]))
    d_enc, enc_grads, enc_gain = block_backward(d_enc, kept_enc, enc_b, norm_gains, 0, geom)
    d_first = d_enc.reshape(-1, C).astype(jnp.bfloat16)
    d_patch = along_rows(pixels, d_first)
    grad_pixel = jnp.stack([reduce_grad(d_patch), reduce_grad(d_head)])
    grad_res = jnp.stack(
        [
            reduce_grad(enc_grads[0]),
            reduce_grad(enc_grads[1]),
            reduce_grad(dec_grads[0]),
            reduce_grad(dec_grads[1]),
        ]
    )
    grad_scale = jnp.stack([reduce_grad(d_down), reduce_grad(d_up)])
    grad_latent = jnp.stack([reduce_grad(d_proj), reduce_grad(d_back)])
    gain_local = jnp.stack(
        [
            enc_gain[0],
            enc_gain[1],
            dec_gain[0],
            dec_gain[1],
            enc_gain[2],
            enc_gain[3],
            dec_gain[2],
            dec_gain[3],
        ]
    )
    grad_gains, smooth_sum, commit_sum = lax.psum((gain_local, l1_local, commit), ("dp", "fsdp"))
    shard_squares = jnp.sum(grad_pixel * grad_pixel) + jnp.sum(grad_res * grad_res)
    shard_squares = (
        shard_squares + jnp.sum(grad_scale * grad_scale) + jnp.sum(grad_latent * grad_latent)
    )
    total_squares = lax.psum(shard_squares, ("dp", "fsdp")) + jnp.sum(grad_gains * grad_gains)
    norm = jnp.sqrt(total_squares)
    factor = CLIP_AT / jnp.maximum(norm, CLIP_AT)
    groups_all = [
        (w_pixel, moment_pixel, second_pixel, grad_pixel),
        (w_res, moment_res, second_res, grad_res),
        (w_scale, moment_scale, second_scale, grad_scale),
        (w_latent, moment_latent, second_latent, grad_latent),
    ]
    outputs = [jnp.stack([smooth_sum, total_valid, commit_sum]), norm.reshape(1)]
    for weight, moment, second, grad in groups_all:
        weight_new, moment_new, second_new = adam_step(
            weight, moment, second, grad * factor, WEIGHT_RATE
        )
        outputs += [weight_new, moment_new, second_new, weight_new.astype(jnp.bfloat16)]
    outputs += list(
        adam_step(norm_gains, moment_gains, second_gains, grad_gains * factor, GAIN_RATE)
    )
    prev = jnp.concatenate([jnp.zeros_like(q_cum[:1]), q_cum[:-1]], axis=0)
    resid = (latent[None] - prev).astype(jnp.bfloat16).reshape(-1, ZD)
    block_len = min(K, 2048)

    def code_block(start):
        onehot = (
            flat_codes[:, None] == start + jnp.arange(block_len, dtype=jnp.int32)[None, :]
        ).astype(jnp.bfloat16)
        return (along_rows(onehot, resid), jnp.sum(onehot, axis=0, dtype=jnp.float32))

    sums_all, counts_all = lax.map(code_block, jnp.arange(0, K, block_len, dtype=jnp.int32))
    sums_all = sums_all.reshape(K, ZD)
    counts_all = counts_all.reshape(K)
    sums_total, counts_total = lax.psum((sums_all, counts_all), ("dp", "fsdp"))
    start_row = lax.axis_index(("dp", "fsdp")) * rows
    my_sums = lax.dynamic_slice_in_dim(sums_total, start_row, rows, 0)
    my_counts = lax.dynamic_slice_in_dim(counts_total, start_row, rows, 0)
    counts_new = EMA_DECAY * ema_counts + (1.0 - EMA_DECAY) * my_counts
    sums_new = EMA_DECAY * ema_sums + (1.0 - EMA_DECAY) * my_sums
    book_new = sums_new / counts_new[:, None]
    outputs += [counts_new, sums_new, book_new, book_new.astype(jnp.bfloat16)]
    return tuple(outputs)


def solution(mesh):
    placed = (
        P(("dp", "fsdp"), None),
        P(("dp", "fsdp"), None),
        P(("dp", "fsdp")),
        P(None, ("dp", "fsdp")),
        P(None, "fsdp", "dp"),
        P(None, "fsdp", "dp"),
        P(None, "fsdp", "dp"),
        P(None, "fsdp", "dp"),
        P(),
        P(None, "fsdp", "dp"),
        P(None, "fsdp", "dp"),
        P(None, "fsdp", "dp"),
        P(None, "fsdp", "dp"),
        P(),
        P(None, "fsdp", "dp"),
        P(None, "fsdp", "dp"),
        P(None, "fsdp", "dp"),
        P(None, "fsdp", "dp"),
        P(),
        P(("dp", "fsdp")),
        P(("dp", "fsdp"), None),
    )
    return jax.shard_map(
        on_device,
        mesh=mesh,
        in_specs=placed,
        out_specs=(
            P(),
            P(),
            P(None, "fsdp", "dp"),
            P(None, "fsdp", "dp"),
            P(None, "fsdp", "dp"),
            P(None, "fsdp", "dp"),
            P(None, "fsdp", "dp"),
            P(None, "fsdp", "dp"),
            P(None, "fsdp", "dp"),
            P(None, "fsdp", "dp"),
            P(None, "fsdp", "dp"),
            P(None, "fsdp", "dp"),
            P(None, "fsdp", "dp"),
            P(None, "fsdp", "dp"),
            P(None, "fsdp", "dp"),
            P(None, "fsdp", "dp"),
            P(None, "fsdp", "dp"),
            P(None, "fsdp", "dp"),
            P(),
            P(),
            P(),
            P(("dp", "fsdp")),
            P(("dp", "fsdp"), None),
            P(("dp", "fsdp"), None),
            P(("dp", "fsdp"), None),
        ),
        check_vma=False,
    )
```

profile of v0, /device:TPU:12, one launch (start us, length us, event | category | flops | bytes accessed | tf_op | source)
XLA Modules:
  0.0 1944.9 jit_solution(17899605121491176382)
XLA Ops:
  11.5 22.5 %all-gather.31.cloned.1.call-done = bf16[1,1152,512]{1,2,0:T(8,128)(2,1)} async-done(((bf16[1,1152,64]{1,2,0:T(8,128)(2,1)}), bf16[1,1152,512]{1,2,0:T(8,128)(2,1)}) %all-gather.31.cloned.1.call-update) | async-done | bytes 1179664 | tf_op jit(solution)/shard_map/all_gather | solution.py:150
  36.5 22.2 %all-gather.35.cloned.1.call-done = bf16[1,1152,512]{1,2,0:T(8,128)(2,1)} async-done(((bf16[1,1152,64]{1,2,0:T(8,128)(2,1)}), bf16[1,1152,512]{1,2,0:T(8,128)(2,1)}) %all-gather.35.cloned.1.call-update) | async-done | bytes 1179664 | tf_op jit(solution)/shard_map/all_gather | solution.py:150
  61.2 15.9 all-gather.6
  77.2 16.3 all-gather.12
  105.0 8.0 while.37
  119.3 15.9 fusion.437
  145.1 5.2 all-to-all-start
  151.1 14.2 all-gather
  165.4 12.4 all-gather.1
  192.5 7.5 gather_fusion.2
  201.3 5.3 all-to-all-start.2
  208.5 29.5 %all-gather.10 = bf16[1,128,256]{1,2,0:T(8,128)(2,1)S(1)} all-gather(bf16[1,128,32]{1,2,0:T(8,128)(2,1)S(1)} %get-tuple-element.455), channel_id=12, replica_groups=mesh['dp'=8,'fsdp'=4] {'dp'}, dimensions={2}, use_global_device_ids=true | all-gather | bytes 73728 | tf_op jit(solution)/shard_map/all_gather | solution.py:150
  238.0 14.3 all-gather.18
  260.5 5.7 all-to-all-start.3
  266.2 15.3 all-gather.8
  287.8 11.7 all-gather.9
  299.5 8.7 all-gather.11
  308.2 12.0 all-gather.19
  320.2 5.5 fusion.150
  327.4 5.0 gather_fusion.3
  364.2 5.3 fusion.158
  419.4 5.1 fusion.166
  445.5 5.4 fusion.174
  464.8 6.6 multiply_reduce_fusion
  471.4 41.4 %psum.50 = f32[]{:T(128)} all-reduce(f32[]{:T(128)} %get-tuple-element.298), channel_id=1, replica_groups=mesh['dp'=8,'fsdp'=4] {'dp','fsdp'}, use_global_device_ids=true, to_apply=%region_27.30 | all-reduce | flops 1 | bytes 8 | tf_op jit(solution)/shard_map/psum | solution.py:217
  512.8 6.2 divide_convert_fusion
  565.6 9.8 fusion.495
  579.8 5.7 fusion.511
  627.8 8.0 fusion.496
  641.4 5.3 fusion.510
  671.8 8.6 fusion.497
  795.2 49.7 %while.36 = (s32[]{:T(128)}, f32[8,2048,256]{2,1,0:T(8,128)}, f32[8,2048]{1,0:T(8,128)S(1)}, s32[4,256]{1,0:T(4,128)S(1)}, s32[8]{0:T(128)S(1)}, /*index=5*/bf16[1024,256]{1,0:T(8,128)(2,1)S(1)}, s32[]{:T(128)}, s32[]{:T(128)}) while((s32[]{:T(128)}, f32[8,2048,256]{2,1,0:T(8,128)}, f32[8,2048]{1,0:T(8,128)S(1)}, s32[4,256]{1,0:T(4,128)S(1)}, ...), condition=%wide.region_84.87_spmd, body=%wide.region_82.86_spmd.sunk | while | flops 1084227584 | bytes 2687093 | solution.py:355
  851.7 95.4 %reduce-scatter.45.cloned.1.call-done = f32[1152,512]{1,0:T(8,128)} async-done(((f32[4608,512]{1,0:T(8,128)}), f32[1152,512]{1,0:T(8,128)}) %reduce-scatter.45.cloned.1.call-update) | async-done | bytes 2359312 | tf_op jit(solution)/shard_map/reduce_scatter | solution.py:159
  950.2 94.9 %reduce-scatter.47.cloned.1.call-done = f32[1152,512]{1,0:T(8,128)} async-done(((f32[4608,512]{1,0:T(8,128)}), f32[1152,512]{1,0:T(8,128)}) %reduce-scatter.47.cloned.1.call-update) | async-done | bytes 2359312 | tf_op jit(solution)/shard_map/reduce_scatter | solution.py:159
  1048.3 95.0 %reduce-scatter.49.cloned.1.call-done = f32[1152,512]{1,0:T(8,128)} async-done(((f32[4608,512]{1,0:T(8,128)}), f32[1152,512]{1,0:T(8,128)}) %reduce-scatter.49.cloned.1.call-update) | async-done | bytes 2359312 | tf_op jit(solution)/shard_map/reduce_scatter | solution.py:159
  1146.4 94.9 %reduce-scatter.51.cloned.1.call-done = f32[1152,512]{1,0:T(8,128)} async-done(((f32[4608,512]{1,0:T(8,128)}), f32[1152,512]{1,0:T(8,128)}) %reduce-scatter.51.cloned.1.call-update) | async-done | bytes 2359312 | tf_op jit(solution)/shard_map/reduce_scatter | solution.py:159
  1245.8 25.0 %reduce-scatter.77.cloned.1.call-done = f32[32,128]{1,0:T(8,128)} async-done(((f32[256,128]{1,0:T(8,128)}), f32[32,128]{1,0:T(8,128)}) %reduce-scatter.77.cloned.1.call-update) | async-done | bytes 16400
  1271.7 30.3 %reduce-scatter.79.cloned.1.call-done = f32[32,128]{1,0:T(8,128)} async-done(((f32[256,128]{1,0:T(8,128)}), f32[32,128]{1,0:T(8,128)}) %reduce-scatter.79.cloned.1.call-update) | async-done | bytes 16400
  1303.5 30.4 %reduce-scatter.43.cloned.1.call-done = f32[192,64]{0,1:T(8,128)} async-done(((f32[192,512]{0,1:T(8,128)}), f32[192,64]{0,1:T(8,128)}) %reduce-scatter.43.cloned.1.call-update) | async-done | bytes 49168 | tf_op jit(solution)/shard_map/reduce_scatter | solution.py:160
  1334.0 31.9 %reduce-scatter.41.cloned.1.call-done = f32[192,64]{0,1:T(8,128)} async-done(((f32[192,512]{0,1:T(8,128)}), f32[192,64]{0,1:T(8,128)}) %reduce-scatter.41.cloned.1.call-update) | async-done | bytes 49168 | tf_op jit(solution)/shard_map/reduce_scatter | solution.py:160
  1367.4 288.5 %all-reduce.41.cloned.1.call-done = (f32[16384]{0:T(1024)}, f32[16384,256]{1,0:T(8,128)}) async-done(((f32[16384]{0:T(1024)}, f32[16384,256]{1,0:T(8,128)}), (f32[16384]{0:T(1024)}, f32[16384,256]{1,0:T(8,128)})) %all-reduce.41.cloned.1.call-update) | async-done | bytes 16842768 | tf_op jit(solution)/shard_map/psum | solution.py:358
  1658.8 28.4 %reduce-scatter.75.cloned.1.call-done = f32[64,512]{1,0:T(8,128)} async-done(((f32[512,512]{1,0:T(8,128)}), f32[64,512]{1,0:T(8,128)}) %reduce-scatter.75.cloned.1.call-update) | async-done | bytes 131088
  1687.2 33.6 %reduce-scatter.73.cloned.1.call-done = f32[64,512]{1,0:T(8,128)} async-done(((f32[512,512]{1,0:T(8,128)}), f32[64,512]{1,0:T(8,128)}) %reduce-scatter.73.cloned.1.call-update) | async-done | bytes 131088
  1722.4 35.2 %reduce-scatter.65.cloned.1.call-done = f32[64,1152]{1,0:T(8,128)} async-done(((f32[512,1152]{1,0:T(8,128)}), f32[64,1152]{1,0:T(8,128)}) %reduce-scatter.65.cloned.1.call-update) | async-done | bytes 294928
  1757.6 37.8 %reduce-scatter.67.cloned.1.call-done = f32[64,1152]{1,0:T(8,128)} async-done(((f32[512,1152]{1,0:T(8,128)}), f32[64,1152]{1,0:T(8,128)}) %reduce-scatter.67.cloned.1.call-update) | async-done | bytes 294928
  1795.4 37.7 %reduce-scatter.69.cloned.1.call-done = f32[64,1152]{1,0:T(8,128)} async-done(((f32[512,1152]{1,0:T(8,128)}), f32[64,1152]{1,0:T(8,128)}) %reduce-scatter.69.cloned.1.call-update) | async-done | bytes 294928
  1833.0 37.8 %reduce-scatter.71.cloned.1.call-done = f32[64,1152]{1,0:T(8,128)} async-done(((f32[512,1152]{1,0:T(8,128)}), f32[64,1152]{1,0:T(8,128)}) %reduce-scatter.71.cloned.1.call-update) | async-done | bytes 294928
  1875.8 44.7 %all-reduce.37 = (f32[1]{0:T(128)}, f32[1]{0:T(128)}, f32[]{:T(128)}, f32[8,512]{1,0:T(8,128)}) all-reduce(f32[1]{0:T(128)} %bitcast.179, f32[1]{0:T(128)} %bitcast.177, f32[]{:T(128)S(6)} %add.1351, f32[8,512]{1,0:T(8,128)} %stack.107), channel_id=1, replica_groups=mesh['dp'=8,'fsdp'=4] {'dp','fsdp'}, use_global_device_ids=true, to_apply=%region_29.32 | all-reduce | flops 4099 | bytes 32792 | tf_op jit(solution)/shard_map/psum | solution.py:322
  (1035 shorter events, 526.1 us)
Async XLA Ops:
  7.2 26.8 %all-gather.31.cloned.1.call-start = ((), (), s32[]{:S(2)}) async-start(), calls=%async_computation.34 | async-start | bytes 1327104 | tf_op jit(solution)/shard_map/all_gather | solution.py:150
  9.4 49.3 %all-gather.35.cloned.1.call-start = ((), (), s32[]{:S(2)}) async-start(), calls=%async_computation.36 | async-start | bytes 1327104 | tf_op jit(solution)/shard_map/all_gather | solution.py:150
  10.2 92.4 %all-gather.43.cloned.1.call-start = ((), (), s32[]{:S(2)}) async-start(), calls=%async_computation.40 | async-start | bytes 1327104 | tf_op jit(solution)/shard_map/all_gather | solution.py:150
  10.9 314.8 %all-gather.47.cloned.1.call-start = ((), (), s32[]{:S(2)}) async-start(), calls=%async_computation.42 | async-start | bytes 1327104 | tf_op jit(solution)/shard_map/all_gather | solution.py:150
  11.5 322.0 %all-gather.33.cloned.1.call-start = ((), (), s32[]{:S(2)}) async-start(), calls=%async_computation.35 | async-start | bytes 5898240 | tf_op jit(solution)/shard_map/all_gather | solution.py:151
  36.4 333.2 %all-gather.37.cloned.1.call-start = ((), (), s32[]{:S(2)}) async-start(), calls=%async_computation.37 | async-start | bytes 5898240 | tf_op jit(solution)/shard_map/all_gather | solution.py:151
  61.1 323.2 %all-gather.39.cloned.1.call-start = ((), (), s32[]{:S(2)}) async-start(), calls=%async_computation.38 | async-start | bytes 2621440 | tf_op jit(solution)/shard_map/all_gather | solution.py:151
  77.2 311.2 %all-gather.41.cloned.1.call-start = ((), (), s32[]{:S(2)}) async-start(), calls=%async_computation.39 | async-start | bytes 2621440 | tf_op jit(solution)/shard_map/all_gather | solution.py:151
  93.5 331.1 %all-gather.45.cloned.1.call-start = ((), (), s32[]{:S(2)}) async-start(), calls=%async_computation.41 | async-start | bytes 5898240 | tf_op jit(solution)/shard_map/all_gather | solution.py:151
  145.1 37.4 %all-to-all-start = ((s32[8,1,256]{2,1,0:T(1,128)}), s32[8,1,256]{2,1,0:T(1,128)S(1)}, u32[]{:S(2)}, u32[]{:S(2)}) async-start(s32[8,1,256]{2,1,0:T(1,128)} %reshape.3897), calls=%async_computation | async-start | bytes 16384 | tf_op jit(solution)/shard_map/all_to_all | solution.py:222
  180.4 104.8 %copy-start.8 = (f32[1024,512]{1,0:T(8,128)}, f32[1024,512]{1,0:T(8,128)S(1)}, u32[]{:S(2)}) copy-start(f32[1024,512]{1,0:T(8,128)S(1)} %fusion.236) | copy-start | bytes 6291460
  184.5 7.1 all-to-all-start.1
  201.3 56.9 %all-to-all-start.2 = ((bf16[8,4,64,256]{3,2,1,0:T(8,128)(2,1)}), bf16[8,4,64,256]{3,2,1,0:T(8,128)(2,1)}, u32[]{:S(2)}, u32[]{:S(2)}) async-start(bf16[8,4,64,256]{3,2,1,0:T(8,128)(2,1)} %broadcast_select_fusion.2), calls=%async_computation.2 | async-start | bytes 2097152 | tf_op jit(solution)/shard_map/all_to_all | solution.py:230
  253.9 66.3 %copy-start.147 = (bf16[32,32]{1,0:T(8,128)(2,1)}, bf16[32,32]{1,0:T(8,128)(2,1)S(1)}, u32[]{:S(2)}) copy-start(bf16[32,32]{1,0:T(8,128)(2,1)S(1)} %get-tuple-element.479) | copy-start | bytes 6148
  253.9 66.3 %copy-start.149 = (bf16[32,32]{1,0:T(8,128)(2,1)}, bf16[32,32]{1,0:T(8,128)(2,1)S(1)}, u32[]{:S(2)}) copy-start(bf16[32,32]{1,0:T(8,128)(2,1)S(1)} %get-tuple-element.484) | copy-start | bytes 6148
  253.9 66.3 %copy-start.151 = (bf16[32,32]{1,0:T(8,128)(2,1)}, bf16[32,32]{1,0:T(8,128)(2,1)S(1)}, u32[]{:S(2)}) copy-start(bf16[32,32]{1,0:T(8,128)(2,1)S(1)} %get-tuple-element.485) | copy-start | bytes 6148
  253.9 66.3 %copy-start.153 = (bf16[32,32]{1,0:T(8,128)(2,1)}, bf16[32,32]{1,0:T(8,128)(2,1)S(1)}, u32[]{:S(2)}) copy-start(bf16[32,32]{1,0:T(8,128)(2,1)S(1)} %get-tuple-element.488) | copy-start | bytes 6148
  260.5 65.4 %all-to-all-start.3 = ((bf16[8,4,64,256]{3,2,0,1:T(8,128)(2,1)}), bf16[8,4,64,256]{3,2,0,1:T(8,128)(2,1)}, u32[]{:S(2)}, u32[]{:S(2)}) async-start(bf16[8,4,64,256]{3,2,0,1:T(8,128)(2,1)} %copy.304), calls=%async_computation.3 | async-start | bytes 2097152 | tf_op jit(solution)/shard_map/all_to_all | solution.py:229
  266.1 184.8 %all-gather.49.cloned.1.call-start = ((), (), s32[]{:S(2)}) async-start(), calls=%async_computation.43 | async-start | bytes 5898240 | tf_op jit(solution)/shard_map/all_gather | solution.py:151
  325.8 461.3 %reduce-scatter.57.cloned.1.call-start = ((), (), s32[]{:S(2)}) async-start(), calls=%async_computation.32 | async-start | bytes 655360 | tf_op jit(solution)/shard_map/reduce_scatter | solution.py:159
  333.5 53.6 %copy-start.42 = (f32[4,256,256]{2,1,0:T(8,128)}, f32[4,256,256]{2,1,0:T(8,128)S(1)}, u32[]{:S(2)}) copy-start(f32[4,256,256]{2,1,0:T(8,128)S(1)} %fusion.175) | copy-start | bytes 3145732
  607.9 181.0 %reduce-scatter.59.cloned.1.call-start = ((), (), s32[]{:S(2)}) async-start(), calls=%async_computation.33 | async-start | bytes 655360 | tf_op jit(solution)/shard_map/reduce_scatter | solution.py:159
  639.8 150.9 %reduce-scatter.63.cloned.1.call-start = ((), (), s32[]{:S(2)}) async-start(), calls=%async_computation.45 | async-start | bytes 1966080
  658.5 134.3 %reduce-scatter.61.cloned.1.call-start = ((), (), s32[]{:S(2)}) async-start(), calls=%async_computation.44 | async-start | bytes 1966080
  707.0 138.6 %reduce-scatter.55.cloned.1.call-start = ((), (), s32[]{:S(2)}) async-start(), calls=%async_computation.31 | async-start | bytes 5242880 | tf_op jit(solution)/shard_map/reduce_scatter | solution.py:159
  709.9 139.1 %reduce-scatter.53.cloned.1.call-start = ((), (), s32[]{:S(2)}) async-start(), calls=%async_computation.30 | async-start | bytes 5242880 | tf_op jit(solution)/shard_map/reduce_scatter | solution.py:159
  714.1 233.0 %reduce-scatter.45.cloned.1.call-start = ((), (), s32[]{:S(2)}) async-start(), calls=%async_computation.26 | async-start | bytes 11796480 | tf_op jit(solution)/shard_map/reduce_scatter | solution.py:159
  730.8 314.3 %reduce-scatter.47.cloned.1.call-start = ((), (), s32[]{:S(2)}) async-start(), calls=%async_computation.27 | async-start | bytes 11796480 | tf_op jit(solution)/shard_map/reduce_scatter | solution.py:159
  748.0 395.2 %reduce-scatter.49.cloned.1.call-start = ((), (), s32[]{:S(2)}) async-start(), calls=%async_computation.28 | async-start | bytes 11796480 | tf_op jit(solution)/shard_map/reduce_scatter | solution.py:159
  769.9 471.4 %reduce-scatter.51.cloned.1.call-start = ((), (), s32[]{:S(2)}) async-start(), calls=%async_computation.29 | async-start | bytes 11796480 | tf_op jit(solution)/shard_map/reduce_scatter | solution.py:159
  787.0 483.9 %reduce-scatter.77.cloned.1.call-start = ((), (), s32[]{:S(2)}) async-start(), calls=%async_computation.52 | async-start | bytes 147456
  788.8 513.2 %reduce-scatter.79.cloned.1.call-start = ((), (), s32[]{:S(2)}) async-start(), calls=%async_computation.53 | async-start | bytes 147456
  790.6 543.4 %reduce-scatter.43.cloned.1.call-start = ((), (), s32[]{:S(2)}) async-start(), calls=%async_computation.25 | async-start | bytes 589824 | tf_op jit(solution)/shard_map/reduce_scatter | solution.py:160
  792.7 573.2 %reduce-scatter.41.cloned.1.call-start = ((), (), s32[]{:S(2)}) async-start(), calls=%async_computation.24 | async-start | bytes 589824 | tf_op jit(solution)/shard_map/reduce_scatter | solution.py:160
  794.8 861.0 %all-reduce.41.cloned.1.call-start = ((), (), s32[]{:S(2)}) async-start(), calls=%async_computation.54 | async-start | bytes 33685504 | tf_op jit(solution)/shard_map/psum | solution.py:358
  845.6 841.6 %reduce-scatter.75.cloned.1.call-start = ((), (), s32[]{:S(2)}) async-start(), calls=%async_computation.51 | async-start | bytes 1179648
  848.2 872.5 %reduce-scatter.73.cloned.1.call-start = ((), (), s32[]{:S(2)}) async-start(), calls=%async_computation.50 | async-start | bytes 1179648
  851.6 905.9 %reduce-scatter.65.cloned.1.call-start = ((), (), s32[]{:S(2)}) async-start(), calls=%async_computation.46 | async-start | bytes 2654208
  950.1 845.2 %reduce-scatter.67.cloned.1.call-start = ((), (), s32[]{:S(2)}) async-start(), calls=%async_computation.47 | async-start | bytes 2654208
  1048.2 784.8 %reduce-scatter.69.cloned.1.call-start = ((), (), s32[]{:S(2)}) async-start(), calls=%async_computation.48 | async-start | bytes 2654208
  1146.4 724.5 %reduce-scatter.71.cloned.1.call-start = ((), (), s32[]{:S(2)}) async-start(), calls=%async_computation.49 | async-start | bytes 2654208
  1244.5 411.4 %copy-start.207 = (f32[512]{0:T(512)S(1)}, f32[512]{0:T(512)}, u32[]{:S(2)}) copy-start(f32[512]{0:T(512)} %param.48) | copy-start | bytes 6148
  1244.5 412.1 %copy-start.120 = (f32[512,256]{1,0:T(8,128)S(1)}, f32[512,256]{1,0:T(8,128)}, u32[]{:S(2)}) copy-start(f32[512,256]{1,0:T(8,128)} %param.49) | copy-start | bytes 1572868
  1302.9 568.0 %copy-start.163 = (f32[1,128,32]{1,2,0:T(8,128)}, f32[1,128,32]{1,2,0:T(8,128)S(1)}, u32[]{:S(2)}) copy-start(f32[1,128,32]{1,2,0:T(8,128)S(1)} %copy.328) | copy-start | bytes 49156
  1656.6 214.3 %copy-start.208 = (f32[512]{0:T(512)}, f32[512]{0:T(512)S(1)}, u32[]{:S(2)}) copy-start(f32[512]{0:T(512)S(1)} %multiply_add_fusion.10) | copy-start | bytes 6148
  1870.9 59.5 %copy-start.46 = (f32[4,1152,64]{1,2,0:T(8,128)S(1)}, f32[4,1152,64]{1,2,0:T(8,128)}, u32[]{:S(2)}) copy-start(f32[4,1152,64]{1,2,0:T(8,128)} %param.34) | copy-start | bytes 3538948
  1870.9 59.5 %copy-start.125 = (f32[4,1152,64]{1,2,0:T(8,128)S(1)}, f32[4,1152,64]{1,2,0:T(8,128)}, u32[]{:S(2)}) copy-start(f32[4,1152,64]{1,2,0:T(8,128)} %param.39) | copy-start | bytes 3538948
  1870.9 59.5 %copy-start.126 = (f32[4,1152,64]{1,2,0:T(8,128)S(1)}, f32[4,1152,64]{1,2,0:T(8,128)}, u32[]{:S(2)}) copy-start(f32[4,1152,64]{1,2,0:T(8,128)} %param.44) | copy-start | bytes 3538948
  (212 other events, 857.9 us)
Sparse Core Ops, SparseCore 0:
  10.2 23.7 all-gather.30
  36.2 22.4 all-gather.34
  60.9 23.7 all-gather.42
  86.8 22.9 all-gather.46
  112.1 56.5 all-gather.32
  171.0 57.1 all-gather.36
  230.0 35.1 all-gather.38
  267.0 40.4 all-gather.40
  310.0 57.5 all-gather.44
  369.3 57.0 all-gather.48
  608.0 24.4 reduce-scatter.56
  639.9 24.4 reduce-scatter.58
  667.4 30.8 reduce-scatter.62
  707.1 30.5 reduce-scatter.60
  740.6 52.6 reduce-scatter.54
  796.3 52.6 reduce-scatter.52
  852.0 94.9 reduce-scatter.44
  950.0 95.0 reduce-scatter.46
  1048.2 95.0 reduce-scatter.48
  1146.2 95.0 reduce-scatter.50
  1244.1 26.7 reduce-scatter.76
  1273.8 28.2 reduce-scatter.78
  1304.9 29.0 reduce-scatter.42
  1336.8 29.0 reduce-scatter.40
  1372.9 282.9 all-reduce.40
  1658.6 28.5 reduce-scatter.74
  1689.9 30.8 reduce-scatter.72
  1723.1 34.4 reduce-scatter.64
  1759.9 35.4 reduce-scatter.66
  1797.5 35.4 reduce-scatter.68
  1835.4 35.4 reduce-scatter.70
where the time goes:
time: 1960 us; the launch traced here: 1940 us
  waiting for transfers between devices  1050 us (54%)
  matrix products  256 us (13%)
  blocking collectives  237 us (12%)
  local copies, waits for them, and re-layouts  188 us (10%)
  other arithmetic  170 us (9%)
  between operations  24.2 us (1%)
  starting transfers between devices  22.2 us (1%)
    reduce_scatter x8, waiting for transfers between devices, reduce_grad(): rows = lax.psum_scatter(full, 'fsdp', scatter_dimension=0, tiled=True)  381 us
    psum x1, waiting for transfers between devices, on_device(): sums_total, counts_total = lax.psum((sums_all, counts_all), ('dp', 'fsdp'))  288 us
    unnamed x41, waiting for transfers between devices  268 us
    all_gather x6, blocking collectives, fetch(): cols = lax.all_gather(shard.astype(jnp.bfloat16), 'dp', axis=1, tiled=True)  106 us
    dot_general x49, matrix products, along_rows(): lax.dot_general(left, right, (((0,), (0,)), ((), ())), preferred_element_...  103 us
    dot_general x41, matrix products, along_cols(): lax.dot_general(left, right, (((1,), (1,)), ((), ())), preferred_element_...  88.1 us
    reduce_scatter x2, waiting for transfers between devices, reduce_grad(): return lax.psum_scatter(rows, 'dp', scatter_dimension=1, tiled=True)  62.3 us
    unnamed x467, local copies, waits for them, and re-layouts  60.6 us
  transfers between devices with their start and end apart: 35, of which 19 were waited for; matrix products, arithmetic and copies ran while one was open for 24% of the time, Pallas kernels for 0%

commit v1 on v0

--- a/solution.py
+++ b/solution.py
@@ -355,7 +355,7 @@
     sums_all, counts_all = lax.map(code_block, jnp.arange(0, K, block_len, dtype=jnp.int32))
     sums_all = sums_all.reshape(K, ZD)
     counts_all = counts_all.reshape(K)
-    sums_total, counts_total = lax.psum((sums_all, counts_all), ("dp", "fsdp"))
+    sums_total, counts_total = lax.psum(lax.psum((sums_all, counts_all), "fsdp"), "dp")
     start_row = lax.axis_index(("dp", "fsdp")) * rows
     my_sums = lax.dynamic_slice_in_dim(sums_total, start_row, rows, 0)
     my_counts = lax.dynamic_slice_in_dim(counts_total, start_row, rows, 0)

time: 1960 us -> 2260 us (1.15)
  waiting for transfers between devices: 1050 us -> 1350 us
    psum x1 -> x2, waiting for transfers between devices: 288 us -> 585 us  [the longest x1 310 us: on_device(): lax.psum((sums_all, counts_all), 'fsdp')]
    unnamed x41 -> x42, waiting for transfers between devices: 268 us -> 275 us
    unnamed x467 -> x471, local copies, waits for them, and re-layouts: 60.6 us -> 61.4 us
  transfers between devices with their start and end apart: 35 -> 36, of which waited for: 19 -> 20; matrix products, arithmetic and copies ran while one was open for 24% -> 21% of each run, Pallas kernels for 0% -> 0%
where the time goes in v1:
time: 2260 us; the launch traced here: 2250 us
  waiting for transfers between devices  1350 us (60%)
  matrix products  256 us (11%)
  blocking collectives  238 us (11%)
  local copies, waits for them, and re-layouts  189 us (8%)
  other arithmetic  170 us (8%)
  between operations  23.9 us (1%)
    reduce_scatter x8, waiting for transfers between devices, reduce_grad(): rows = lax.psum_scatter(full, 'fsdp', scatter_dimension=0, tiled=True)  380 us
    psum x1, waiting for transfers between devices, on_device(): lax.psum((sums_all, counts_all), 'fsdp')  310 us
    unnamed x42, waiting for transfers between devices  275 us
    psum x1, waiting for transfers between devices, on_device(): lax.psum(lax.psum((sums_all, counts_all), 'fsdp'), 'dp')  275 us
    all_gather x6, blocking collectives, fetch(): cols = lax.all_gather(shard.astype(jnp.bfloat16), 'dp', axis=1, tiled=True)  105 us
    dot_general x49, matrix products, along_rows(): lax.dot_general(left, right, (((0,), (0,)), ((), ())), preferred_element_...  103 us
    dot_general x41, matrix products, along_cols(): lax.dot_general(left, right, (((1,), (1,)), ((), ())), preferred_element_...  87.8 us
    reduce_scatter x2, waiting for transfers between devices, reduce_grad(): return lax.psum_scatter(rows, 'dp', scatter_dimension=1, tiled=True)  62.3 us
  transfers between devices with their start and end apart: 36, of which 20 were waited for; matrix products, arithmetic and copies ran while one was open for 21% of the time, Pallas kernels for 0%

profile of v1, /device:TPU:12, one launch (start us, length us, event | category | flops | bytes accessed | tf_op | source)
XLA Modules:
  0.0 2249.8 jit_solution(12234728035799786868)
XLA Ops:
  11.5 22.5 all-gather.31.cloned.1.call-done
  36.5 22.2 all-gather.35.cloned.1.call-done
  61.2 15.9 all-gather.6
  77.2 16.3 all-gather.12
  105.0 8.0 while.37
  119.2 15.8 fusion.437
  145.0 5.2 all-to-all-start
  150.9 14.2 all-gather
  165.3 12.4 all-gather.1
  192.4 7.5 gather_fusion.2
  201.2 5.2 all-to-all-start.2
  208.3 29.5 %all-gather.10 = bf16[1,128,256]{1,2,0:T(8,128)(2,1)S(1)} all-gather(bf16[1,128,32]{1,2,0:T(8,128)(2,1)S(1)} %get-tuple-element.457), channel_id=12, replica_groups=mesh['dp'=8,'fsdp'=4] {'dp'}, dimensions={2}, use_global_device_ids=true | all-gather | bytes 73728 | tf_op jit(solution)/shard_map/all_gather | solution.py:150
  237.9 14.3 all-gather.18
  260.3 5.8 all-to-all-start.3
  266.1 15.2 all-gather.8
  287.6 11.5 all-gather.9
  299.1 9.0 all-gather.11
  308.1 12.0 all-gather.19
  320.1 5.4 fusion.150
  364.0 5.3 fusion.158
  419.2 5.2 fusion.166
  445.3 5.4 fusion.174
  464.6 6.5 multiply_reduce_fusion
  471.2 41.7 %psum.64 = f32[]{:T(128)} all-reduce(f32[]{:T(128)} %get-tuple-element.298), channel_id=1, replica_groups=mesh['dp'=8,'fsdp'=4] {'dp','fsdp'}, use_global_device_ids=true, to_apply=%region_27.30 | all-reduce | flops 1 | bytes 8 | tf_op jit(solution)/shard_map/psum | solution.py:217
  512.9 6.2 divide_convert_fusion
  565.6 9.8 fusion.495
  579.9 5.7 fusion.511
  627.8 7.9 fusion.496
  641.4 5.3 fusion.510
  671.7 8.5 fusion.497
  787.9 49.7 %while.36 = (s32[]{:T(128)}, f32[8,2048,256]{2,1,0:T(8,128)}, f32[8,2048]{1,0:T(8,128)S(1)}, s32[4,256]{1,0:T(4,128)S(1)}, s32[8]{0:T(128)S(1)}, /*index=5*/bf16[1024,256]{1,0:T(8,128)(2,1)S(1)}, s32[]{:T(128)}, s32[]{:T(128)}) while((s32[]{:T(128)}, f32[8,2048,256]{2,1,0:T(8,128)}, f32[8,2048]{1,0:T(8,128)S(1)}, s32[4,256]{1,0:T(4,128)S(1)}, ...), condition=%wide.region_84.87_spmd, body=%wide.region_82.86_spmd.sunk | while | flops 1084227584 | bytes 2687093 | solution.py:355
  851.6 95.4 %reduce-scatter.45.cloned.1.call-done = f32[1152,512]{1,0:T(8,128)} async-done(((f32[4608,512]{1,0:T(8,128)}), f32[1152,512]{1,0:T(8,128)}) %reduce-scatter.45.cloned.1.call-update) | async-done | bytes 2359312 | tf_op jit(solution)/shard_map/reduce_scatter | solution.py:159
  950.1 94.9 %reduce-scatter.47.cloned.1.call-done = f32[1152,512]{1,0:T(8,128)} async-done(((f32[4608,512]{1,0:T(8,128)}), f32[1152,512]{1,0:T(8,128)}) %reduce-scatter.47.cloned.1.call-update) | async-done | bytes 2359312 | tf_op jit(solution)/shard_map/reduce_scatter | solution.py:159
  1048.2 95.0 %reduce-scatter.49.cloned.1.call-done = f32[1152,512]{1,0:T(8,128)} async-done(((f32[4608,512]{1,0:T(8,128)}), f32[1152,512]{1,0:T(8,128)}) %reduce-scatter.49.cloned.1.call-update) | async-done | bytes 2359312 | tf_op jit(solution)/shard_map/reduce_scatter | solution.py:159
  1146.3 94.9 %reduce-scatter.51.cloned.1.call-done = f32[1152,512]{1,0:T(8,128)} async-done(((f32[4608,512]{1,0:T(8,128)}), f32[1152,512]{1,0:T(8,128)}) %reduce-scatter.51.cloned.1.call-update) | async-done | bytes 2359312 | tf_op jit(solution)/shard_map/reduce_scatter | solution.py:159
  1244.4 310.0 %all-reduce.45.cloned.1.call-done = (f32[16384]{0:T(1024)}, f32[16384,256]{1,0:T(8,128)}) async-done(((f32[16384]{0:T(1024)}, f32[16384,256]{1,0:T(8,128)}), (f32[16384]{0:T(1024)}, f32[16384,256]{1,0:T(8,128)})) %all-reduce.45.cloned.1.call-update) | async-done | bytes 16842768 | tf_op jit(solution)/shard_map/psum | solution.py:358
  1555.8 28.7 %reduce-scatter.77.cloned.1.call-done = f32[32,128]{1,0:T(8,128)} async-done(((f32[256,128]{1,0:T(8,128)}), f32[32,128]{1,0:T(8,128)}) %reduce-scatter.77.cloned.1.call-update) | async-done | bytes 16400
  1585.4 30.2 %reduce-scatter.79.cloned.1.call-done = f32[32,128]{1,0:T(8,128)} async-done(((f32[256,128]{1,0:T(8,128)}), f32[32,128]{1,0:T(8,128)}) %reduce-scatter.79.cloned.1.call-update) | async-done | bytes 16400
  1617.1 30.4 %reduce-scatter.43.cloned.1.call-done = f32[192,64]{0,1:T(8,128)} async-done(((f32[192,512]{0,1:T(8,128)}), f32[192,64]{0,1:T(8,128)}) %reduce-scatter.43.cloned.1.call-update) | async-done | bytes 49168 | tf_op jit(solution)/shard_map/reduce_scatter | solution.py:160
  1647.5 31.9 %reduce-scatter.41.cloned.1.call-done = f32[192,64]{0,1:T(8,128)} async-done(((f32[192,512]{0,1:T(8,128)}), f32[192,64]{0,1:T(8,128)}) %reduce-scatter.41.cloned.1.call-update) | async-done | bytes 49168 | tf_op jit(solution)/shard_map/reduce_scatter | solution.py:160
  1680.9 31.8 %reduce-scatter.75.cloned.1.call-done = f32[64,512]{1,0:T(8,128)} async-done(((f32[512,512]{1,0:T(8,128)}), f32[64,512]{1,0:T(8,128)}) %reduce-scatter.75.cloned.1.call-update) | async-done | bytes 131088
  1712.7 33.1 %reduce-scatter.73.cloned.1.call-done = f32[64,512]{1,0:T(8,128)} async-done(((f32[512,512]{1,0:T(8,128)}), f32[64,512]{1,0:T(8,128)}) %reduce-scatter.73.cloned.1.call-update) | async-done | bytes 131088
  1747.5 35.6 %reduce-scatter.65.cloned.1.call-done = f32[64,1152]{1,0:T(8,128)} async-done(((f32[512,1152]{1,0:T(8,128)}), f32[64,1152]{1,0:T(8,128)}) %reduce-scatter.65.cloned.1.call-update) | async-done | bytes 294928
  1783.0 37.9 %reduce-scatter.67.cloned.1.call-done = f32[64,1152]{1,0:T(8,128)} async-done(((f32[512,1152]{1,0:T(8,128)}), f32[64,1152]{1,0:T(8,128)}) %reduce-scatter.67.cloned.1.call-update) | async-done | bytes 294928
  1820.9 37.8 %reduce-scatter.69.cloned.1.call-done = f32[64,1152]{1,0:T(8,128)} async-done(((f32[512,1152]{1,0:T(8,128)}), f32[64,1152]{1,0:T(8,128)}) %reduce-scatter.69.cloned.1.call-update) | async-done | bytes 294928
  1858.7 37.9 %reduce-scatter.71.cloned.1.call-done = f32[64,1152]{1,0:T(8,128)} async-done(((f32[512,1152]{1,0:T(8,128)}), f32[64,1152]{1,0:T(8,128)}) %reduce-scatter.71.cloned.1.call-update) | async-done | bytes 294928
  1901.5 46.2 %all-reduce.37 = (f32[1]{0:T(128)}, f32[1]{0:T(128)}, f32[]{:T(128)}, f32[8,512]{1,0:T(8,128)}) all-reduce(f32[1]{0:T(128)} %bitcast.179, f32[1]{0:T(128)} %bitcast.177, f32[]{:T(128)S(6)} %add.1355, f32[8,512]{1,0:T(8,128)} %stack.107), channel_id=1, replica_groups=mesh['dp'=8,'fsdp'=4] {'dp','fsdp'}, use_global_device_ids=true, to_apply=%region_29.32 | all-reduce | flops 4099 | bytes 32792 | tf_op jit(solution)/shard_map/psum | solution.py:322
  1964.0 274.7 %all-reduce.43.cloned.1.call-done = (f32[16384]{0:T(1024)}, f32[16384,256]{1,0:T(8,128)}) async-done(((f32[16384]{0:T(1024)}, f32[16384,256]{1,0:T(8,128)}), (f32[16384]{0:T(1024)}, f32[16384,256]{1,0:T(8,128)})) %all-reduce.43.cloned.1.call-update) | async-done | bytes 16842768 | tf_op jit(solution)/shard_map/psum | solution.py:358
  (1042 shorter events, 531.5 us)
Async XLA Ops:
  7.2 26.8 %all-gather.31.cloned.1.call-start = ((), (), s32[]{:S(2)}) async-start(), calls=%async_computation.34 | async-start | bytes 1327104 | tf_op jit(solution)/shard_map/all_gather | solution.py:150
  9.4 49.3 %all-gather.35.cloned.1.call-start = ((), (), s32[]{:S(2)}) async-start(), calls=%async_computation.36 | async-start | bytes 1327104 | tf_op jit(solution)/shard_map/all_gather | solution.py:150
  10.2 92.4 %all-gather.43.cloned.1.call-start = ((), (), s32[]{:S(2)}) async-start(), calls=%async_computation.40 | async-start | bytes 1327104 | tf_op jit(solution)/shard_map/all_gather | solution.py:150
  10.9 314.6 %all-gather.47.cloned.1.call-start = ((), (), s32[]{:S(2)}) async-start(), calls=%async_computation.42 | async-start | bytes 1327104 | tf_op jit(solution)/shard_map/all_gather | solution.py:150
  11.5 321.9 %all-gather.33.cloned.1.call-start = ((), (), s32[]{:S(2)}) async-start(), calls=%async_computation.35 | async-start | bytes 5898240 | tf_op jit(solution)/shard_map/all_gather | solution.py:151
  36.4 332.9 %all-gather.37.cloned.1.call-start = ((), (), s32[]{:S(2)}) async-start(), calls=%async_computation.37 | async-start | bytes 5898240 | tf_op jit(solution)/shard_map/all_gather | solution.py:151
  61.1 323.0 %all-gather.39.cloned.1.call-start = ((), (), s32[]{:S(2)}) async-start(), calls=%async_computation.38 | async-start | bytes 2621440 | tf_op jit(solution)/shard_map/all_gather | solution.py:151
  77.2 311.0 %all-gather.41.cloned.1.call-start = ((), (), s32[]{:S(2)}) async-start(), calls=%async_computation.39 | async-start | bytes 2621440 | tf_op jit(solution)/shard_map/all_gather | solution.py:151
  93.5 330.9 %all-gather.45.cloned.1.call-start = ((), (), s32[]{:S(2)}) async-start(), calls=%async_computation.41 | async-start | bytes 5898240 | tf_op jit(solution)/shard_map/all_gather | solution.py:151
  145.0 37.4 %all-to-all-start = ((s32[8,1,256]{2,1,0:T(1,128)}), s32[8,1,256]{2,1,0:T(1,128)S(1)}, u32[]{:S(2)}, u32[]{:S(2)}) async-start(s32[8,1,256]{2,1,0:T(1,128)} %reshape.3897), calls=%async_computation | async-start | bytes 16384 | tf_op jit(solution)/shard_map/all_to_all | solution.py:222
  180.3 104.8 %copy-start.8 = (f32[1024,512]{1,0:T(8,128)}, f32[1024,512]{1,0:T(8,128)S(1)}, u32[]{:S(2)}) copy-start(f32[1024,512]{1,0:T(8,128)S(1)} %fusion.236) | copy-start | bytes 6291460
  184.4 7.1 all-to-all-start.1
  201.2 56.8 %all-to-all-start.2 = ((bf16[8,4,64,256]{3,2,1,0:T(8,128)(2,1)}), bf16[8,4,64,256]{3,2,1,0:T(8,128)(2,1)}, u32[]{:S(2)}, u32[]{:S(2)}) async-start(bf16[8,4,64,256]{3,2,1,0:T(8,128)(2,1)} %broadcast_select_fusion.2), calls=%async_computation.2 | async-start | bytes 2097152 | tf_op jit(solution)/shard_map/all_to_all | solution.py:230
  253.8 66.3 %copy-start.148 = (bf16[32,32]{1,0:T(8,128)(2,1)}, bf16[32,32]{1,0:T(8,128)(2,1)S(1)}, u32[]{:S(2)}) copy-start(bf16[32,32]{1,0:T(8,128)(2,1)S(1)} %get-tuple-element.481) | copy-start | bytes 6148
  253.8 66.3 %copy-start.150 = (bf16[32,32]{1,0:T(8,128)(2,1)}, bf16[32,32]{1,0:T(8,128)(2,1)S(1)}, u32[]{:S(2)}) copy-start(bf16[32,32]{1,0:T(8,128)(2,1)S(1)} %get-tuple-element.486) | copy-start | bytes 6148
  253.8 66.3 %copy-start.152 = (bf16[32,32]{1,0:T(8,128)(2,1)}, bf16[32,32]{1,0:T(8,128)(2,1)S(1)}, u32[]{:S(2)}) copy-start(bf16[32,32]{1,0:T(8,128)(2,1)S(1)} %get-tuple-element.487) | copy-start | bytes 6148
  253.8 66.3 %copy-start.154 = (bf16[32,32]{1,0:T(8,128)(2,1)}, bf16[32,32]{1,0:T(8,128)(2,1)S(1)}, u32[]{:S(2)}) copy-start(bf16[32,32]{1,0:T(8,128)(2,1)S(1)} %get-tuple-element.490) | copy-start | bytes 6148
  260.3 65.3 %all-to-all-start.3 = ((bf16[8,4,64,256]{3,2,0,1:T(8,128)(2,1)}), bf16[8,4,64,256]{3,2,0,1:T(8,128)(2,1)}, u32[]{:S(2)}, u32[]{:S(2)}) async-start(bf16[8,4,64,256]{3,2,0,1:T(8,128)(2,1)} %copy.304), calls=%async_computation.3 | async-start | bytes 2097152 | tf_op jit(solution)/shard_map/all_to_all | solution.py:229
  266.1 184.6 %all-gather.49.cloned.1.call-start = ((), (), s32[]{:S(2)}) async-start(), calls=%async_computation.43 | async-start | bytes 5898240 | tf_op jit(solution)/shard_map/all_gather | solution.py:151
  325.6 512.8 %reduce-scatter.57.cloned.1.call-start = ((), (), s32[]{:S(2)}) async-start(), calls=%async_computation.32 | async-start | bytes 655360 | tf_op jit(solution)/shard_map/reduce_scatter | solution.py:159
  607.9 232.2 %reduce-scatter.59.cloned.1.call-start = ((), (), s32[]{:S(2)}) async-start(), calls=%async_computation.33 | async-start | bytes 655360 | tf_op jit(solution)/shard_map/reduce_scatter | solution.py:159
  639.7 202.2 %reduce-scatter.63.cloned.1.call-start = ((), (), s32[]{:S(2)}) async-start(), calls=%async_computation.45 | async-start | bytes 1966080
  658.4 185.5 %reduce-scatter.61.cloned.1.call-start = ((), (), s32[]{:S(2)}) async-start(), calls=%async_computation.44 | async-start | bytes 1966080
  706.9 139.2 %reduce-scatter.55.cloned.1.call-start = ((), (), s32[]{:S(2)}) async-start(), calls=%async_computation.31 | async-start | bytes 5242880 | tf_op jit(solution)/shard_map/reduce_scatter | solution.py:159
  709.8 139.2 %reduce-scatter.53.cloned.1.call-start = ((), (), s32[]{:S(2)}) async-start(), calls=%async_computation.30 | async-start | bytes 5242880 | tf_op jit(solution)/shard_map/reduce_scatter | solution.py:159
  713.9 233.1 %reduce-scatter.45.cloned.1.call-start = ((), (), s32[]{:S(2)}) async-start(), calls=%async_computation.26 | async-start | bytes 11796480 | tf_op jit(solution)/shard_map/reduce_scatter | solution.py:159
  730.7 314.3 %reduce-scatter.47.cloned.1.call-start = ((), (), s32[]{:S(2)}) async-start(), calls=%async_computation.27 | async-start | bytes 11796480 | tf_op jit(solution)/shard_map/reduce_scatter | solution.py:159
  747.9 395.3 %reduce-scatter.49.cloned.1.call-start = ((), (), s32[]{:S(2)}) async-start(), calls=%async_computation.28 | async-start | bytes 11796480 | tf_op jit(solution)/shard_map/reduce_scatter | solution.py:159
  769.7 471.5 %reduce-scatter.51.cloned.1.call-start = ((), (), s32[]{:S(2)}) async-start(), calls=%async_computation.29 | async-start | bytes 11796480 | tf_op jit(solution)/shard_map/reduce_scatter | solution.py:159
  786.9 767.4 %all-reduce.45.cloned.1.call-start = ((), (), s32[]{:S(2)}) async-start(), calls=%async_computation.55 | async-start | bytes 33685504 | tf_op jit(solution)/shard_map/psum | solution.py:358
  838.3 746.2 %reduce-scatter.77.cloned.1.call-start = ((), (), s32[]{:S(2)}) async-start(), calls=%async_computation.52 | async-start | bytes 147456
  840.1 775.5 %reduce-scatter.79.cloned.1.call-start = ((), (), s32[]{:S(2)}) async-start(), calls=%async_computation.53 | async-start | bytes 147456
  841.8 805.7 %reduce-scatter.43.cloned.1.call-start = ((), (), s32[]{:S(2)}) async-start(), calls=%async_computation.25 | async-start | bytes 589824 | tf_op jit(solution)/shard_map/reduce_scatter | solution.py:160
  843.9 835.5 %reduce-scatter.41.cloned.1.call-start = ((), (), s32[]{:S(2)}) async-start(), calls=%async_computation.24 | async-start | bytes 589824 | tf_op jit(solution)/shard_map/reduce_scatter | solution.py:160
  846.0 866.7 %reduce-scatter.75.cloned.1.call-start = ((), (), s32[]{:S(2)}) async-start(), calls=%async_computation.51 | async-start | bytes 1179648
  848.7 897.2 %reduce-scatter.73.cloned.1.call-start = ((), (), s32[]{:S(2)}) async-start(), calls=%async_computation.50 | async-start | bytes 1179648
  851.5 931.5 %reduce-scatter.65.cloned.1.call-start = ((), (), s32[]{:S(2)}) async-start(), calls=%async_computation.46 | async-start | bytes 2654208
  950.1 870.8 %reduce-scatter.67.cloned.1.call-start = ((), (), s32[]{:S(2)}) async-start(), calls=%async_computation.47 | async-start | bytes 2654208
  1048.1 810.5 %reduce-scatter.69.cloned.1.call-start = ((), (), s32[]{:S(2)}) async-start(), calls=%async_computation.48 | async-start | bytes 2654208
  1146.3 750.3 %reduce-scatter.71.cloned.1.call-start = ((), (), s32[]{:S(2)}) async-start(), calls=%async_computation.49 | async-start | bytes 2654208
  1244.3 994.4 %all-reduce.43.cloned.1.call-start = ((), (), s32[]{:S(2)}) async-start(), calls=%async_computation.54 | async-start | bytes 33685504 | tf_op jit(solution)/shard_map/psum | solution.py:358
  1554.4 398.5 %copy-start.187 = (f32[8,512]{1,0:T(8,128)S(1)}, f32[8,512]{1,0:T(8,128)}, u32[]{:S(2)}) copy-start(f32[8,512]{1,0:T(8,128)} %param.37) | copy-start | bytes 49156
  1554.4 399.9 %copy-start.165 = (f32[2,128,32]{1,2,0:T(8,128)S(1)}, f32[2,128,32]{1,2,0:T(8,128)}, u32[]{:S(2)}) copy-start(f32[2,128,32]{1,2,0:T(8,128)} %param.36) | copy-start | bytes 98308
  1554.4 401.3 %copy-start.138 = (f32[2,192,64]{1,2,0:T(8,128)S(1)}, f32[2,192,64]{1,2,0:T(8,128)}, u32[]{:S(2)}) copy-start(f32[2,192,64]{1,2,0:T(8,128)} %param.33) | copy-start | bytes 294916
  1554.5 403.1 %copy-start.131 = (f32[2,512,64]{1,2,0:T(8,128)S(1)}, f32[2,512,64]{1,2,0:T(8,128)}, u32[]{:S(2)}) copy-start(f32[2,512,64]{1,2,0:T(8,128)} %param.35) | copy-start | bytes 786436
  1712.7 244.9 %copy-start.139 = (f32[64,512]{1,0:T(8,128)S(1)}, f32[64,512]{1,0:T(8,128)}, u32[]{:S(2)}) copy-start(f32[64,512]{1,0:T(8,128)} %reduce-scatter.75.cloned.1.call-done) | copy-start | bytes 393220
  1959.8 279.0 %copy-start.209 = (f32[512]{0:T(512)S(1)}, f32[512]{0:T(512)}, u32[]{:S(2)}) copy-start(f32[512]{0:T(512)} %param.48) | copy-start | bytes 6148
  1959.8 279.7 %copy-start.120 = (f32[512,256]{1,0:T(8,128)S(1)}, f32[512,256]{1,0:T(8,128)}, u32[]{:S(2)}) copy-start(f32[512,256]{1,0:T(8,128)} %param.49) | copy-start | bytes 1572868
  (215 other events, 1130.3 us)
Sparse Core Ops, SparseCore 0:
  10.2 23.7 all-gather.30
  36.2 22.4 all-gather.34
  60.9 23.7 all-gather.42
  86.8 22.9 all-gather.46
  112.1 56.5 all-gather.32
  171.0 57.2 all-gather.36
  230.1 35.1 all-gather.38
  267.1 40.3 all-gather.40
  309.9 57.5 all-gather.44
  369.2 57.0 all-gather.48
  608.0 24.4 reduce-scatter.56
  639.9 24.4 reduce-scatter.58
  667.3 30.9 reduce-scatter.62
  707.0 30.6 reduce-scatter.60
  740.5 52.6 reduce-scatter.54
  796.3 52.6 reduce-scatter.52
  851.9 95.0 reduce-scatter.44
  950.0 95.0 reduce-scatter.46
  1048.1 95.0 reduce-scatter.48
  1146.1 95.0 reduce-scatter.50
  1245.5 308.8 all-reduce.44
  1557.2 27.2 reduce-scatter.76
  1587.3 28.2 reduce-scatter.78
  1618.4 29.0 reduce-scatter.42
  1650.3 29.0 reduce-scatter.40
  1682.2 30.4 reduce-scatter.74
  1715.5 30.2 reduce-scatter.72
  1748.2 34.7 reduce-scatter.64
  1785.5 35.3 reduce-scatter.66
  1823.2 35.4 reduce-scatter.68
  1861.1 35.4 reduce-scatter.70
  1899.4 339.2 all-reduce.42
